TPU v7x, 32 devices: a whole 2x2x4 slice. The times are simulated.
32 devices in a mesh: blk: 16 (over z, x, core), rep: 2 (over y).
Axes of the slice: x: 2, y: 2, z: 4, core: 2. Of those that a mesh axis runs over, the one named last changes fastest.
Arguments:
- features: bfloat16 [4096, 128], P(('blk', 'rep')), may hold values from -6 to 6
- tile_mask: int32 [32, 32], P('blk'), may hold values 0 or 1
- multiplicity: int32 [32, 32], P('blk'), may hold values from 1 to 4
- w_query: bfloat16 [128, 128], replicated, may hold values from -0.5 to 0.5
- w_value: bfloat16 [128, 128], replicated, may hold values from -0.5 to 0.5
Outputs:
- updated: bfloat16 [4096, 128], P(('blk', 'rep'))
All inputs are finite; a program needn't handle non-finite values. No bound on the sum of `tile_mask` on one device may be relied on, other than what follows from the above.
Results may differ from a plain program's by a relative error of at most 0.0057.
Values may be sent and summed in bfloat16 or wider, within the bound.
A program may use at most 64 MiB of HBM per device.

v0:
```python
import math
import jax
import jax.numpy as jnp
from jax import lax
from jax.sharding import PartitionSpec as P

TILE = 128


def body(features, tile_mask, multiplicity, w_query, w_value):
    src_rows = features.shape[0]
    cycle_count = lax.axis_size("blk")
    rep_count = lax.axis_size("rep")
    rep_index = lax.axis_index("rep")
    own_query = jnp.dot(features, w_query, preferred_element_type=jnp.float32).astype(jnp.bfloat16)
    queries = lax.all_gather(own_query, "rep", axis=0, tiled=True)
    tgt_rows = queries.shape[0]
    tgt_tiles = tgt_rows // TILE
    src_tiles = src_rows // TILE
    factor = (tile_mask * multiplicity).astype(jnp.float32)
    factor = factor.reshape(tgt_tiles, cycle_count, rep_count, src_tiles)
    factor = lax.dynamic_index_in_dim(factor, rep_index, 2, keepdims=False)
    root_scale = 1.0 / features.shape[1] ** 0.5

    def absorb_tiles(partial_value, source, tile_factor):
        count_rows = source.shape[0]
        scores = (
            lax.dot_general(
                queries, source, (((1,), (1,)), ((), ())), preferred_element_type=jnp.float32
            )
            * root_scale
        )
        scores = jnp.where(scores > 0, scores, 0.2 * scores)
        weights = (
            scores.reshape(tgt_tiles, TILE, count_rows // TILE, TILE)
            * tile_factor[:, None, :, None]
        )
        weights = weights.reshape(tgt_rows, count_rows).astype(jnp.bfloat16)
        return partial_value + jnp.dot(weights, source, preferred_element_type=jnp.float32)

    start = jnp.zeros((tgt_rows, features.shape[1]), jnp.float32)
    flat_factor = factor.reshape(tgt_tiles, cycle_count * src_tiles)
    piece = lax.all_gather(features, "blk", axis=0, tiled=True)
    piece_rows = piece.shape[0]
    step_rows = math.gcd(piece_rows, max(src_rows, 1024))
    step_count = piece_rows // step_rows
    piece_blocks = piece.reshape(step_count, step_rows, piece.shape[1])

    def one_part(carry, index_pair):
        part_rows, part_index = index_pair
        first_tile = part_index * step_rows // TILE
        tile_factor = lax.dynamic_slice_in_dim(flat_factor, first_tile, step_rows // TILE, 1)
        return (absorb_tiles(carry, part_rows, tile_factor), None)

    result, unused = lax.scan(
        one_part, start, (piece_blocks, jnp.arange(step_count, dtype=jnp.int32))
    )
    partial_value = result
    summed = lax.psum_scatter(partial_value, "rep", scatter_dimension=0, tiled=True)
    total_verts = src_rows * cycle_count * rep_count
    aggregate = (summed * (2.0 * total_verts) ** (-0.5)).astype(jnp.bfloat16)
    mixed = jnp.dot(aggregate, w_value, preferred_element_type=jnp.float32)
    return (features.astype(jnp.float32) + mixed).astype(jnp.bfloat16)


def solution(mesh):
    in_specs = (P(("blk", "rep"), None), P("blk", None), P("blk", None), P(), P())
    out_specs = P(("blk", "rep"), None)
    return jax.shard_map(body, mesh=mesh, in_specs=in_specs, out_specs=out_specs, check_vma=False)
```

profile of v0, /device:TPU:0, one launch (start us, length us, event | category | flops | bytes accessed | tf_op | source)
XLA Modules:
  0.0 58.8 jit_solution(14389451639451653202)
XLA Ops:
  6.5 0.0 copy-start
  6.5 0.0 reduce-scatter.2.cloned.1.call-start
  6.6 0.7 %copy-done.5 = s32[2,32]{1,0:T(2,128)S(1)} copy-done((s32[2,32]{1,0:T(2,128)S(1)}, s32[2,32]{1,0:T(2,128)}, u32[]{:S(2)}) %copy-start.5) | copy-done | bytes 280
  7.2 0.0 copy-done.4
  7.3 0.1 reshape.20
  7.3 0.1 constant_dynamic-slice_fusion.1
  7.4 0.2 copy.8
  7.6 0.5 copy-done.1
  8.1 24.6 %all_gather.6 = bf16[2048,128]{1,0:T(8,128)(2,1)S(1)} all-gather(bf16[128,128]{1,0:T(8,128)(2,1)S(1)} %copy-done.1), channel_id=1, replica_groups=mesh['blk'=16,'rep'=2] {'blk'}, dimensions={0}, use_global_device_ids=true | all-gather | bytes 557056 | tf_op jit(solution)/shard_map/all_gather | solution.py:43
  32.7 0.0 copy-done
  32.7 0.1 convolution_convert_fusion
  32.8 4.6 %all_gather.7 = bf16[256,128]{1,0:T(8,128)(2,1)S(1)} all-gather(bf16[128,128]{1,0:T(8,128)(2,1)S(1)} %convolution_convert_fusion), channel_id=1, replica_groups=mesh['blk'=16,'rep'=2] {'rep'}, dimensions={0}, use_global_device_ids=true | all-gather | bytes 98304 | tf_op jit(solution)/shard_map/all_gather | solution.py:16
  37.4 4.4 %while.13 = (s32[]{:T(128)}, f32[256,128]{1,0:T(8,128)S(1)}, bf16[2,1024,128]{2,1,0:T(8,128)(2,1)S(1)}, bf16[256,128]{1,0:T(8,128)(2,1)S(1)}, s32[2]{0:T(128)S(1...) while((s32[]{:T(128)}, f32[256,128]{1,0:T(8,128)S(1)}, ...), condition=%wide.region_1.2_spmd.clone, body=%wide.region_0.1_spmd.clone.sunk | while | flops 135856144 | bytes 2950683 | solution.py:55
  37.4 0.6 dynamic_slice.44
  38.6 0.3 mul.98
  38.9 0.7 %convolution_add_fusion.3 = f32[256,128]{1,0:T(8,128)S(1)} fusion(f32[128,8,2,128]{3,2,1,0:T(2,128)S(1)} %bitcast.43, bf16[256,128]{1,0:T(8,128)(2,1)S(1)} %get-tuple-element.196, bf16[2,1024,128]{2,1,0:T(8,128)(2,1)S(1)} %get-tuple-element.195, s32[]{:T(128)} %get-tuple-element.180, f32[256,128]{1,0:T(8,128)S(1)} %get-tuple-element.181, pred[]{:T(512)S(6)} %compare.9), kind=kOutput, calls=%fused_computation.1.clone.1 | convolution fusion | flops 135856128 | bytes 1901569 | tf_op jit(solution)/shard_map/while/body/eval_jaxpr/dot_general | solution.py:39
  39.6 0.6 dynamic_slice.44
  40.8 0.3 mul.98
  41.2 0.7 %convolution_add_fusion.3 = f32[256,128]{1,0:T(8,128)S(1)} fusion(f32[128,8,2,128]{3,2,1,0:T(2,128)S(1)} %bitcast.43, bf16[256,128]{1,0:T(8,128)(2,1)S(1)} %get-tuple-element.196, bf16[2,1024,128]{2,1,0:T(8,128)(2,1)S(1)} %get-tuple-element.195, s32[]{:T(128)} %get-tuple-element.180, f32[256,128]{1,0:T(8,128)S(1)} %get-tuple-element.181, pred[]{:T(512)S(6)} %compare.9), kind=kOutput, calls=%fused_computation.1.clone.1 | convolution fusion | flops 135856128 | bytes 1901569 | tf_op jit(solution)/shard_map/while/body/eval_jaxpr/dot_general | solution.py:39
  41.9 0.0 copy-start.3
  41.9 0.6 %copy-done.2 = f32[256,128]{1,0:T(8,128)} copy-done((f32[256,128]{1,0:T(8,128)}, f32[256,128]{1,0:T(8,128)S(1)}, u32[]{:S(2)}) %copy-start.2) | copy-done | bytes 131096
  42.5 0.0 reduce-scatter.2.cloned.1.call-update
  42.5 7.8 %reduce-scatter.2.cloned.1.call-done = f32[128,128]{1,0:T(8,128)} async-done(((f32[256,128]{1,0:T(8,128)}), f32[128,128]{1,0:T(8,128)}) %reduce-scatter.2.cloned.1.call-update) | async-done | bytes 65552 | tf_op jit(solution)/shard_map/reduce_scatter | solution.py:59
  50.3 1.6 %fusion.14 = bf16[128,128]{1,0:T(8,128)(2,1)} fusion(bf16[128,128]{1,0:T(8,128)(2,1)S(1)} %copy-done.3, bf16[128,128]{1,0:T(8,128)(2,1)S(1)} %copy-done.1, f32[128,128]{1,0:T(8,128)} %reduce-scatter.2.cloned.1.call-done), kind=kOutput, calls=%fused_computation.15 | convolution fusion | flops 4276224 | bytes 163840 | tf_op jit(solution)/shard_map/dot_general | solution.py:62
  (10 shorter events, 0.0 us)
Async XLA Ops:
  6.5 26.2 %copy-start = (bf16[128,128]{1,0:T(8,128)(2,1)S(1)}, bf16[128,128]{1,0:T(8,128)(2,1)}, u32[]{:S(2)}) copy-start(bf16[128,128]{1,0:T(8,128)(2,1)} %param.10) | copy-start | bytes 98308
  6.5 43.8 %reduce-scatter.2.cloned.1.call-start = ((), (), s32[]{:S(2)}) async-start(), calls=%async_computation.1 | async-start | bytes 196608 | tf_op jit(solution)/shard_map/reduce_scatter | solution.py:59
  6.5 0.7 %copy-start.5 = (s32[2,32]{1,0:T(2,128)S(1)}, s32[2,32]{1,0:T(2,128)}, u32[]{:S(2)}) copy-start(s32[2,32]{1,0:T(2,128)} %param.9) | copy-start | bytes 772
  6.5 0.7 %copy-start.4 = (s32[2,32]{1,0:T(2,128)S(1)}, s32[2,32]{1,0:T(2,128)}, u32[]{:S(2)}) copy-start(s32[2,32]{1,0:T(2,128)} %param.8) | copy-start | bytes 772
  7.3 0.8 %copy-start.1 = (bf16[128,128]{1,0:T(8,128)(2,1)S(1)}, bf16[128,128]{1,0:T(8,128)(2,1)}, u32[]{:S(2)}) copy-start(bf16[128,128]{1,0:T(8,128)(2,1)} %param.7) | copy-start | bytes 98308
  41.8 0.7 %copy-start.2 = (f32[256,128]{1,0:T(8,128)}, f32[256,128]{1,0:T(8,128)S(1)}, u32[]{:S(2)}) copy-start(f32[256,128]{1,0:T(8,128)S(1)} %get-tuple-element.84) | copy-start | bytes 393220
  41.9 8.5 %copy-start.3 = (bf16[128,128]{1,0:T(8,128)(2,1)S(1)}, bf16[128,128]{1,0:T(8,128)(2,1)}, u32[]{:S(2)}) copy-start(bf16[128,128]{1,0:T(8,128)(2,1)} %param.11) | copy-start | bytes 98308
Sparse Core Ops, SparseCore 0:
  42.6 7.6 reduce-scatter.1
where the time goes:
time: 59.1 us; the launch traced here: 58.8 us
  blocking collectives  29.2 us (49%)
  between operations  13.4 us (23%)
  waiting for transfers between devices  7.82 us (13%)
  local copies, waits for them, and re-layouts  4.05 us (7%)
  matrix products  3.05 us (5%)
  loops' own time  1.24 us (2%)
    all_gather x1, blocking collectives, body(): piece = lax.all_gather(features, 'blk', axis=0, tiled=True)  24.6 us
    reduce_scatter x1, waiting for transfers between devices, body(): lax.psum_scatter(partial_value, 'rep', scatter_dimension=0, tiled=True)  7.8 us
    all_gather x1, blocking collectives, body(): queries = lax.all_gather(own_query, 'rep', axis=0, tiled=True)  4.58 us
    unnamed x13, local copies, waits for them, and re-layouts  2.02 us
    dot_general x1, matrix products, body(): mixed = jnp.dot(aggregate, w_value, preferred_element_type=jnp.float32)  1.59 us
    dot_general x2, matrix products, absorb_tiles(): jnp.dot(weights, source, preferred_element_type=jnp.float32)  1.33 us
    another operation x1, loops' own time, body(): lax.scan(one_part, start, (piece_blocks, jnp.arange(step_count, dtype=jnp...  1.24 us
  transfers between devices with their start and end apart: 1, of which 1 were waited for; matrix products, arithmetic and copies ran while one was open for 0% of the time, Pallas kernels for 0%

commit v1 on v0

--- a/solution.py
+++ b/solution.py
@@ -40,7 +40,12 @@
 
     start = jnp.zeros((tgt_rows, features.shape[1]), jnp.float32)
     flat_factor = factor.reshape(tgt_tiles, cycle_count * src_tiles)
-    piece = lax.all_gather(features, "blk", axis=0, tiled=True)
+    ring = [features]
+    for hop in range(15):
+        ring.append(lax.ppermute(ring[-1], "blk", [(dev, (dev + 1) % 16) for dev in range(16)]))
+    piece = jnp.roll(
+        jnp.concatenate(ring[::-1], axis=0), (lax.axis_index("blk") + 1) * ring[0].shape[0], axis=0
+    )
     piece_rows = piece.shape[0]
     step_rows = math.gcd(piece_rows, max(src_rows, 1024))
     step_count = piece_rows // step_rows

time: 59.1 us -> 124 us (2.10)
  waiting for transfers between devices: 7.82 us -> 95.3 us
  blocking collectives: 29.2 us -> 4.57 us
    ppermute x0 -> x15, waiting for transfers between devices: none -> 85.4 us  [body(): lax.ppermute(ring[-1], 'blk', [(dev, (dev + 1) % 16) for dev in range(16)])]
    all_gather x1 -> x0, blocking collectives: 24.6 us -> none  [body(): piece = lax.all_gather(features, 'blk', axis=0, tiled=True)]
    reduce_scatter x1, waiting for transfers between devices: 7.8 us -> 9.85 us  [body(): lax.psum_scatter(partial_value, 'rep', scatter_dimension=0, tiled=True)]
  transfers between devices with their start and end apart: 1 -> 16, of which waited for: 1 -> 16; matrix products, arithmetic and copies ran while one was open for 0% -> 1% of each run, Pallas kernels for 0% -> 0%
where the time goes in v1:
time: 124 us; the launch traced here: 123 us
  waiting for transfers between devices  95.3 us (77%)
  between operations  13.6 us (11%)
  blocking collectives  4.57 us (4%)
  local copies, waits for them, and re-layouts  4.04 us (3%)
  matrix products  3.81 us (3%)
  loops' own time  1.4 us (1%)
    ppermute x15, waiting for transfers between devices, body(): lax.ppermute(ring[-1], 'blk', [(dev, (dev + 1) % 16) for dev in range(16)])  85.4 us
    reduce_scatter x1, waiting for transfers between devices, body(): lax.psum_scatter(partial_value, 'rep', scatter_dimension=0, tiled=True)  9.85 us
    all_gather x1, blocking collectives, body(): queries = lax.all_gather(own_query, 'rep', axis=0, tiled=True)  4.57 us
  transfers between devices with their start and end apart: 16, of which 16 were waited for; matrix products, arithmetic and copies ran while one was open for 1% of the time, Pallas kernels for 0%

profile of v1, /device:TPU:0, one launch (start us, length us, event | category | flops | bytes accessed | tf_op | source)
XLA Modules:
  0.0 123.3 jit_solution(4713297066377542574)
XLA Ops:
  7.1 6.8 %collective-permute-done = bf16[128,128]{1,0:T(8,128)(2,1)S(1)} collective-permute-done((bf16[128,128]{1,0:T(8,128)(2,1)}, bf16[128,128]{1,0:T(8,128)(2,1)S(1)}, u32[]{:S(2)}, u32[]{:S(2)}) %collective-permute-start) | collective-permute-done | bytes 32800 | tf_op jit(solution)/shard_map/ppermute | solution.py:45
  13.9 6.0 %collective-permute-done.1 = bf16[128,128]{1,0:T(8,128)(2,1)S(1)} collective-permute-done((bf16[128,128]{1,0:T(8,128)(2,1)S(1)}, bf16[128,128]{1,0:T(8,128)(2,1)S(1)}, u32[]{:S(2)}, u32[]{:S(2)}) %collective-permute-start.1) | collective-permute-done | bytes 32800 | tf_op jit(solution)/shard_map/ppermute | solution.py:45
  19.9 6.0 %collective-permute-done.2 = bf16[128,128]{1,0:T(8,128)(2,1)S(1)} collective-permute-done((bf16[128,128]{1,0:T(8,128)(2,1)S(1)}, bf16[128,128]{1,0:T(8,128)(2,1)S(1)}, u32[]{:S(2)}, u32[]{:S(2)}) %collective-permute-start.2) | collective-permute-done | bytes 32800 | tf_op jit(solution)/shard_map/ppermute | solution.py:45
  25.9 6.0 %collective-permute-done.3 = bf16[128,128]{1,0:T(8,128)(2,1)S(1)} collective-permute-done((bf16[128,128]{1,0:T(8,128)(2,1)S(1)}, bf16[128,128]{1,0:T(8,128)(2,1)S(1)}, u32[]{:S(2)}, u32[]{:S(2)}) %collective-permute-start.3) | collective-permute-done | bytes 32800 | tf_op jit(solution)/shard_map/ppermute | solution.py:45
  32.0 6.0 %collective-permute-done.4 = bf16[128,128]{1,0:T(8,128)(2,1)S(1)} collective-permute-done((bf16[128,128]{1,0:T(8,128)(2,1)S(1)}, bf16[128,128]{1,0:T(8,128)(2,1)S(1)}, u32[]{:S(2)}, u32[]{:S(2)}) %collective-permute-start.4) | collective-permute-done | bytes 32800 | tf_op jit(solution)/shard_map/ppermute | solution.py:45
  38.0 6.0 %collective-permute-done.5 = bf16[128,128]{1,0:T(8,128)(2,1)S(1)} collective-permute-done((bf16[128,128]{1,0:T(8,128)(2,1)S(1)}, bf16[128,128]{1,0:T(8,128)(2,1)S(1)}, u32[]{:S(2)}, u32[]{:S(2)}) %collective-permute-start.5) | collective-permute-done | bytes 32800 | tf_op jit(solution)/shard_map/ppermute | solution.py:45
  44.0 6.0 %collective-permute-done.6 = bf16[128,128]{1,0:T(8,128)(2,1)S(1)} collective-permute-done((bf16[128,128]{1,0:T(8,128)(2,1)S(1)}, bf16[128,128]{1,0:T(8,128)(2,1)S(1)}, u32[]{:S(2)}, u32[]{:S(2)}) %collective-permute-start.6) | collective-permute-done | bytes 32800 | tf_op jit(solution)/shard_map/ppermute | solution.py:45
  50.1 6.0 %collective-permute-done.7 = bf16[128,128]{1,0:T(8,128)(2,1)S(1)} collective-permute-done((bf16[128,128]{1,0:T(8,128)(2,1)S(1)}, bf16[128,128]{1,0:T(8,128)(2,1)S(1)}, u32[]{:S(2)}, u32[]{:S(2)}) %collective-permute-start.7) | collective-permute-done | bytes 32800 | tf_op jit(solution)/shard_map/ppermute | solution.py:45
  56.1 6.0 %collective-permute-done.8 = bf16[128,128]{1,0:T(8,128)(2,1)S(1)} collective-permute-done((bf16[128,128]{1,0:T(8,128)(2,1)S(1)}, bf16[128,128]{1,0:T(8,128)(2,1)S(1)}, u32[]{:S(2)}, u32[]{:S(2)}) %collective-permute-start.8) | collective-permute-done | bytes 32800 | tf_op jit(solution)/shard_map/ppermute | solution.py:45
  62.2 6.0 %collective-permute-done.9 = bf16[128,128]{1,0:T(8,128)(2,1)S(1)} collective-permute-done((bf16[128,128]{1,0:T(8,128)(2,1)S(1)}, bf16[128,128]{1,0:T(8,128)(2,1)S(1)}, u32[]{:S(2)}, u32[]{:S(2)}) %collective-permute-start.9) | collective-permute-done | bytes 32800 | tf_op jit(solution)/shard_map/ppermute | solution.py:45
  68.2 6.0 %collective-permute-done.10 = bf16[128,128]{1,0:T(8,128)(2,1)S(1)} collective-permute-done((bf16[128,128]{1,0:T(8,128)(2,1)S(1)}, bf16[128,128]{1,0:T(8,128)(2,1)S(1)}, u32[]{:S(2)}, u32[]{:S(2)}) %collective-permute-start.10) | collective-permute-done | bytes 32800 | tf_op jit(solution)/shard_map/ppermute | solution.py:45
  74.2 6.0 %collective-permute-done.11 = bf16[128,128]{1,0:T(8,128)(2,1)S(1)} collective-permute-done((bf16[128,128]{1,0:T(8,128)(2,1)S(1)}, bf16[128,128]{1,0:T(8,128)(2,1)S(1)}, u32[]{:S(2)}, u32[]{:S(2)}) %collective-permute-start.11) | collective-permute-done | bytes 32800 | tf_op jit(solution)/shard_map/ppermute | solution.py:45
  80.3 0.9 convolution_convert_fusion
  81.2 5.1 %collective-permute-done.12 = bf16[128,128]{1,0:T(8,128)(2,1)S(1)} collective-permute-done((bf16[128,128]{1,0:T(8,128)(2,1)S(1)}, bf16[128,128]{1,0:T(8,128)(2,1)S(1)}, u32[]{:S(2)}, u32[]{:S(2)}) %collective-permute-start.12) | collective-permute-done | bytes 32800 | tf_op jit(solution)/shard_map/ppermute | solution.py:45
  86.4 5.9 %collective-permute-done.13 = bf16[128,128]{1,0:T(8,128)(2,1)S(1)} collective-permute-done((bf16[128,128]{1,0:T(8,128)(2,1)S(1)}, bf16[128,128]{1,0:T(8,128)(2,1)S(1)}, u32[]{:S(2)}, u32[]{:S(2)}) %collective-permute-start.13) | collective-permute-done | bytes 32800 | tf_op jit(solution)/shard_map/ppermute | solution.py:45
  92.6 4.6 %all_gather.3 = bf16[256,128]{1,0:T(8,128)(2,1)S(1)} all-gather(bf16[128,128]{1,0:T(8,128)(2,1)S(1)} %convolution_convert_fusion), channel_id=1, replica_groups=mesh['blk'=16,'rep'=2] {'rep'}, dimensions={0}, use_global_device_ids=true | all-gather | bytes 98304 | tf_op jit(solution)/shard_map/all_gather | solution.py:16
  97.2 1.2 collective-permute-done.14
  98.6 0.7 copy-done.1
  99.6 4.7 %while.13 = (s32[]{:T(128)}, f32[256,128]{1,0:T(8,128)S(1)}, bf16[2,1024,128]{2,1,0:T(8,128)(2,1)S(1)}, bf16[256,128]{1,0:T(8,128)(2,1)S(1)}, s32[2]{0:T(128)S(1...) while((s32[]{:T(128)}, f32[256,128]{1,0:T(8,128)S(1)}, ...), condition=%wide.region_1.2_spmd.clone, body=%wide.region_0.1_spmd.clone.sunk | while | flops 135856144 | bytes 2950683 | solution.py:60
  101.3 0.7 convolution_add_fusion.3
  103.6 0.7 convolution_add_fusion.3
  104.3 0.6 copy-done.2
  105.0 9.8 %reduce-scatter.2.cloned.1.call-done = f32[128,128]{1,0:T(8,128)} async-done(((f32[256,128]{1,0:T(8,128)}), f32[128,128]{1,0:T(8,128)}) %reduce-scatter.2.cloned.1.call-update) | async-done | bytes 65552 | tf_op jit(solution)/shard_map/reduce_scatter | solution.py:64
  114.8 1.6 %fusion.14 = bf16[128,128]{1,0:T(8,128)(2,1)} fusion(bf16[128,128]{1,0:T(8,128)(2,1)S(1)} %copy-done.3, bf16[128,128]{1,0:T(8,128)(2,1)S(1)} %copy-done.1, f32[128,128]{1,0:T(8,128)} %reduce-scatter.2.cloned.1.call-done), kind=kOutput, calls=%fused_computation.15 | convolution fusion | flops 4276224 | bytes 163840 | tf_op jit(solution)/shard_map/dot_general | solution.py:67
  (72 shorter events, 3.3 us)
Async XLA Ops:
  6.5 73.7 %copy-start = (bf16[128,128]{1,0:T(8,128)(2,1)S(1)}, bf16[128,128]{1,0:T(8,128)(2,1)}, u32[]{:S(2)}) copy-start(bf16[128,128]{1,0:T(8,128)(2,1)} %param.10) | copy-start | bytes 98308
  6.5 79.8 %copy-start.4 = (s32[2,32]{1,0:T(2,128)S(1)}, s32[2,32]{1,0:T(2,128)}, u32[]{:S(2)}) copy-start(s32[2,32]{1,0:T(2,128)} %param.8) | copy-start | bytes 772
  6.5 79.8 %copy-start.5 = (s32[2,32]{1,0:T(2,128)S(1)}, s32[2,32]{1,0:T(2,128)}, u32[]{:S(2)}) copy-start(s32[2,32]{1,0:T(2,128)} %param.9) | copy-start | bytes 772
  6.5 108.3 %reduce-scatter.2.cloned.1.call-start = ((), (), s32[]{:S(2)}) async-start(), calls=%async_computation.1 | async-start | bytes 196608 | tf_op jit(solution)/shard_map/reduce_scatter | solution.py:64
  6.5 7.3 %collective-permute-start = (bf16[128,128]{1,0:T(8,128)(2,1)}, bf16[128,128]{1,0:T(8,128)(2,1)S(1)}, u32[]{:S(2)}, u32[]{:S(2)}) collective-permute-start(bf16[128,128]{1,0:T(8,128)(2,1)} %param.7), channel_id=1, source_target_pairs={{0,2},{2,4},{4,6},{6,8},{8,10},{10,12},{12,14},{14,16},{16,18},{18... | collective-permute-start | bytes 98312 | tf_op jit(solution)/shard_map/ppermute | solution.py:45
  13.9 6.0 %collective-permute-start.1 = (bf16[128,128]{1,0:T(8,128)(2,1)S(1)}, bf16[128,128]{1,0:T(8,128)(2,1)S(1)}, u32[]{:S(2)}, u32[]{:S(2)}) collective-permute-start(bf16[128,128]{1,0:T(8,128)(2,1)S(1)} %collective-permute-done), channel_id=1, source_target_pairs={{0,2},{2,4},{4,6},{6,8},{8,10},{10,12},{12,14},{14,16},{16,18},{18... | collective-permute-start | bytes 98312 | tf_op jit(solution)/shard_map/ppermute | solution.py:45
  19.9 6.0 %collective-permute-start.2 = (bf16[128,128]{1,0:T(8,128)(2,1)S(1)}, bf16[128,128]{1,0:T(8,128)(2,1)S(1)}, u32[]{:S(2)}, u32[]{:S(2)}) collective-permute-start(bf16[128,128]{1,0:T(8,128)(2,1)S(1)} %collective-permute-done.1), channel_id=1, source_target_pairs={{0,2},{2,4},{4,6},{6,8},{8,10},{10,12},{12,14},{14,16},{16,18},{18... | collective-permute-start | bytes 98312 | tf_op jit(solution)/shard_map/ppermute | solution.py:45
  25.9 6.0 %collective-permute-start.3 = (bf16[128,128]{1,0:T(8,128)(2,1)S(1)}, bf16[128,128]{1,0:T(8,128)(2,1)S(1)}, u32[]{:S(2)}, u32[]{:S(2)}) collective-permute-start(bf16[128,128]{1,0:T(8,128)(2,1)S(1)} %collective-permute-done.2), channel_id=1, source_target_pairs={{0,2},{2,4},{4,6},{6,8},{8,10},{10,12},{12,14},{14,16},{16,18},{18... | collective-permute-start | bytes 98312 | tf_op jit(solution)/shard_map/ppermute | solution.py:45
  32.0 6.0 %collective-permute-start.4 = (bf16[128,128]{1,0:T(8,128)(2,1)S(1)}, bf16[128,128]{1,0:T(8,128)(2,1)S(1)}, u32[]{:S(2)}, u32[]{:S(2)}) collective-permute-start(bf16[128,128]{1,0:T(8,128)(2,1)S(1)} %collective-permute-done.3), channel_id=1, source_target_pairs={{0,2},{2,4},{4,6},{6,8},{8,10},{10,12},{12,14},{14,16},{16,18},{18... | collective-permute-start | bytes 98312 | tf_op jit(solution)/shard_map/ppermute | solution.py:45
  38.0 6.0 %collective-permute-start.5 = (bf16[128,128]{1,0:T(8,128)(2,1)S(1)}, bf16[128,128]{1,0:T(8,128)(2,1)S(1)}, u32[]{:S(2)}, u32[]{:S(2)}) collective-permute-start(bf16[128,128]{1,0:T(8,128)(2,1)S(1)} %collective-permute-done.4), channel_id=1, source_target_pairs={{0,2},{2,4},{4,6},{6,8},{8,10},{10,12},{12,14},{14,16},{16,18},{18... | collective-permute-start | bytes 98312 | tf_op jit(solution)/shard_map/ppermute | solution.py:45
  44.0 6.0 %collective-permute-start.6 = (bf16[128,128]{1,0:T(8,128)(2,1)S(1)}, bf16[128,128]{1,0:T(8,128)(2,1)S(1)}, u32[]{:S(2)}, u32[]{:S(2)}) collective-permute-start(bf16[128,128]{1,0:T(8,128)(2,1)S(1)} %collective-permute-done.5), channel_id=1, source_target_pairs={{0,2},{2,4},{4,6},{6,8},{8,10},{10,12},{12,14},{14,16},{16,18},{18... | collective-permute-start | bytes 98312 | tf_op jit(solution)/shard_map/ppermute | solution.py:45
  50.1 6.0 %collective-permute-start.7 = (bf16[128,128]{1,0:T(8,128)(2,1)S(1)}, bf16[128,128]{1,0:T(8,128)(2,1)S(1)}, u32[]{:S(2)}, u32[]{:S(2)}) collective-permute-start(bf16[128,128]{1,0:T(8,128)(2,1)S(1)} %collective-permute-done.6), channel_id=1, source_target_pairs={{0,2},{2,4},{4,6},{6,8},{8,10},{10,12},{12,14},{14,16},{16,18},{18... | collective-permute-start | bytes 98312 | tf_op jit(solution)/shard_map/ppermute | solution.py:45
  56.1 6.0 %collective-permute-start.8 = (bf16[128,128]{1,0:T(8,128)(2,1)S(1)}, bf16[128,128]{1,0:T(8,128)(2,1)S(1)}, u32[]{:S(2)}, u32[]{:S(2)}) collective-permute-start(bf16[128,128]{1,0:T(8,128)(2,1)S(1)} %collective-permute-done.7), channel_id=1, source_target_pairs={{0,2},{2,4},{4,6},{6,8},{8,10},{10,12},{12,14},{14,16},{16,18},{18... | collective-permute-start | bytes 98312 | tf_op jit(solution)/shard_map/ppermute | solution.py:45
  62.2 6.0 %collective-permute-start.9 = (bf16[128,128]{1,0:T(8,128)(2,1)S(1)}, bf16[128,128]{1,0:T(8,128)(2,1)S(1)}, u32[]{:S(2)}, u32[]{:S(2)}) collective-permute-start(bf16[128,128]{1,0:T(8,128)(2,1)S(1)} %collective-permute-done.8), channel_id=1, source_target_pairs={{0,2},{2,4},{4,6},{6,8},{8,10},{10,12},{12,14},{14,16},{16,18},{18... | collective-permute-start | bytes 98312 | tf_op jit(solution)/shard_map/ppermute | solution.py:45
  68.2 6.0 %collective-permute-start.10 = (bf16[128,128]{1,0:T(8,128)(2,1)S(1)}, bf16[128,128]{1,0:T(8,128)(2,1)S(1)}, u32[]{:S(2)}, u32[]{:S(2)}) collective-permute-start(bf16[128,128]{1,0:T(8,128)(2,1)S(1)} %collective-permute-done.9), channel_id=1, source_target_pairs={{0,2},{2,4},{4,6},{6,8},{8,10},{10,12},{12,14},{14,16},{16,18},{18... | collective-permute-start | bytes 98312 | tf_op jit(solution)/shard_map/ppermute | solution.py:45
  74.2 6.0 %collective-permute-start.11 = (bf16[128,128]{1,0:T(8,128)(2,1)S(1)}, bf16[128,128]{1,0:T(8,128)(2,1)S(1)}, u32[]{:S(2)}, u32[]{:S(2)}) collective-permute-start(bf16[128,128]{1,0:T(8,128)(2,1)S(1)} %collective-permute-done.10), channel_id=1, source_target_pairs={{0,2},{2,4},{4,6},{6,8},{8,10},{10,12},{12,14},{14,16},{16,18},{18... | collective-permute-start | bytes 98312 | tf_op jit(solution)/shard_map/ppermute | solution.py:45
  80.3 6.0 %collective-permute-start.12 = (bf16[128,128]{1,0:T(8,128)(2,1)S(1)}, bf16[128,128]{1,0:T(8,128)(2,1)S(1)}, u32[]{:S(2)}, u32[]{:S(2)}) collective-permute-start(bf16[128,128]{1,0:T(8,128)(2,1)S(1)} %collective-permute-done.11), channel_id=1, source_target_pairs={{0,2},{2,4},{4,6},{6,8},{8,10},{10,12},{12,14},{14,16},{16,18},{18... | collective-permute-start | bytes 98312 | tf_op jit(solution)/shard_map/ppermute | solution.py:45
  86.3 6.0 %collective-permute-start.13 = (bf16[128,128]{1,0:T(8,128)(2,1)S(1)}, bf16[128,128]{1,0:T(8,128)(2,1)S(1)}, u32[]{:S(2)}, u32[]{:S(2)}) collective-permute-start(bf16[128,128]{1,0:T(8,128)(2,1)S(1)} %collective-permute-done.12), channel_id=1, source_target_pairs={{0,2},{2,4},{4,6},{6,8},{8,10},{10,12},{12,14},{14,16},{16,18},{18... | collective-permute-start | bytes 98312 | tf_op jit(solution)/shard_map/ppermute | solution.py:45
  92.3 6.0 %collective-permute-start.14 = (bf16[128,128]{1,0:T(8,128)(2,1)S(1)}, bf16[128,128]{1,0:T(8,128)(2,1)S(1)}, u32[]{:S(2)}, u32[]{:S(2)}) collective-permute-start(bf16[128,128]{1,0:T(8,128)(2,1)S(1)} %collective-permute-done.13), channel_id=1, source_target_pairs={{0,2},{2,4},{4,6},{6,8},{8,10},{10,12},{12,14},{14,16},{16,18},{18... | collective-permute-start | bytes 98312 | tf_op jit(solution)/shard_map/ppermute | solution.py:45
  98.6 0.8 copy-start.1
  104.3 0.7 copy-start.2
  104.3 10.5 %copy-start.3 = (bf16[128,128]{1,0:T(8,128)(2,1)S(1)}, bf16[128,128]{1,0:T(8,128)(2,1)}, u32[]{:S(2)}) copy-start(bf16[128,128]{1,0:T(8,128)(2,1)} %param.11) | copy-start | bytes 98308
Sparse Core Ops, SparseCore 0:
  105.1 9.6 reduce-scatter.1
